TPU v7x, 768 devices: a whole 4x8x12 slice. The times are simulated.
768 devices in a mesh: dp: 8 (over y), row: 8 (over z_lo, core), col: 12 (over x, z_hi).
Axes of the slice: x: 4, y: 8, z: 12 (z_hi: 3, z_lo: 4; z = z_hi * 4 + z_lo), core: 2. Of those that a mesh axis runs over, the one named last changes fastest.
Arguments:
- inputs: bfloat16 [12288, 6144], P('dp', 'row'), may hold values from -6 to 6
- pre_act: bfloat16 [12288, 12288], P(('dp', 'row'), 'col'), may hold values from -8 to 8
- out_grad: bfloat16 [12288, 12288], P(('dp', 'row'), 'col'), may hold values from -6 to 6
- weight: bfloat16 [6144, 12288], P('row', 'col'), may hold values from -6 to 6
- swag_mean: float32 [8, 768, 12288], P('dp', 'row', 'col'), may hold values from -6 to 6
- swag_square: float32 [8, 768, 12288], P('dp', 'row', 'col'), may hold values from 0.5 to 3
- snapshots: int32 [1], replicated, may hold values from 1 to 32
- update_flag: int32 [8, 768], P('dp', 'row'), may hold values 0 or 1
Outputs:
- input_grad: bfloat16 [12288, 6144], P(('dp', 'col'), 'row')
- new_weight: float32 [8, 768, 12288], P('dp', 'row', 'col')
- mean_out: float32 [8, 768, 12288], P('dp', 'row', 'col')
- square_out: float32 [8, 768, 12288], P('dp', 'row', 'col')
All inputs are finite; a program needn't handle non-finite values. No bound on the sum of `update_flag` on one device may be relied on, other than what follows from the above.
Results may differ from a plain program's by a relative error of at most 0.013.
Values may be sent and summed in bfloat16 or wider, within the bound.
A program may use at most 64 MiB of HBM per device.

v0:
```python
import jax
import jax.numpy as jnp
from jax import lax
from jax.sharding import PartitionSpec as P

D = 6144


learning_rate = 0.5


def gelu_slope(values):
    normal_cdf = 0.5 * (1.0 + lax.erf(values * 0.7071067811865476))
    density = jnp.exp(-0.5 * values * values) * 0.3989422804014327
    return normal_cdf + values * density


def body(inputs, pre_act, out_grad, weight, swag_mean, swag_square, snapshots, update_flag):
    replica_tokens = inputs.shape[0]
    row_width = weight.shape[0]
    groups = lax.axis_size("dp")
    share_rows = row_width // groups
    multiplier = 1.0 / D**0.5
    local_grad = (out_grad.astype(jnp.float32) * gelu_slope(pre_act.astype(jnp.float32))).astype(
        jnp.bfloat16
    )
    portion = lax.all_gather(local_grad, "row", axis=0, tiled=True)
    grad_acc = lax.dot_general(
        inputs, portion, (((0,), (0,)), ((), ())), preferred_element_type=jnp.float32
    )
    term_rows = (
        lax.dot_general(
            portion, weight, (((1,), (1,)), ((), ())), preferred_element_type=jnp.float32
        )
        * multiplier
    )
    input_grad = lax.psum_scatter(
        term_rows.astype(jnp.bfloat16), "col", scatter_dimension=0, tiled=True
    )
    replica_index = lax.axis_index("dp")
    summed = lax.psum(grad_acc.astype(jnp.bfloat16), "dp").astype(jnp.float32)
    share = lax.dynamic_slice_in_dim(summed, replica_index * share_rows, share_rows, 0)
    own_rows = lax.dynamic_slice_in_dim(weight, replica_index * share_rows, share_rows, 0).astype(
        jnp.float32
    )
    total_tokens = replica_tokens * groups
    stepped = own_rows - learning_rate * (share / total_tokens**0.5)
    blend = update_flag[0].astype(jnp.float32)[:, None] / (snapshots[0].astype(jnp.float32) + 1.0)
    mean_old = swag_mean[0]
    square_old = swag_square[0]
    mean_new = mean_old + blend * (stepped - mean_old)
    square_new = square_old + blend * (stepped * stepped - square_old)
    return (input_grad, stepped[None], mean_new[None], square_new[None])


def solution(mesh):
    in_specs = (
        P("dp", "row"),
        P(("dp", "row"), "col"),
        P(("dp", "row"), "col"),
        P("row", "col"),
        P("dp", "row", "col"),
        P("dp", "row", "col"),
        P(),
        P("dp", "row"),
    )
    out_specs = (
        P(("dp", "col"), "row"),
        P("dp", "row", "col"),
        P("dp", "row", "col"),
        P("dp", "row", "col"),
    )
    return jax.shard_map(body, mesh=mesh, in_specs=in_specs, out_specs=out_specs, check_vma=False)
```

profile of v0, /device:TPU:6, one launch (start us, length us, event | category | flops | bytes accessed | tf_op | source)
XLA Modules:
  0.0 362.2 jit_solution(2803704866393322225)
XLA Ops:
  7.2 0.0 copy-start
  7.2 0.0 all-gather.2.cloned.1.call-start
  7.2 2.4 fusion.8
  9.6 0.0 all-gather.2.cloned.1.call-update
  9.6 0.0 all-reduce.2.cloned.1.call-start
  9.7 58.4 %all-gather.2.cloned.1.call-done = bf16[1536,1024]{1,0:T(8,128)(2,1)} async-done(((bf16[192,1024]{1,0:T(8,128)(2,1)}), bf16[1536,1024]{1,0:T(8,128)(2,1)}) %all-gather.2.cloned.1.call-update) | async-done | bytes 3145744 | tf_op jit(solution)/shard_map/all_gather | solution.py:27
  68.1 0.0 copy-done
  68.1 5.8 %fusion = bf16[768,1024]{0,1:T(8,128)(2,1)} fusion(bf16[1536,1024]{1,0:T(8,128)(2,1)} %all-gather.2.cloned.1.call-done, bf16[1536,768]{1,0:T(8,128)(2,1)S(1)} %copy-done), kind=kOutput, calls=%fused_computation.2 | convolution fusion | flops 2416705536 | bytes 7077888 | tf_op jit(solution)/shard_map/dot_general | solution.py:28
  73.9 0.0 all-reduce.2.cloned.1.call-update
  73.9 0.0 reduce-scatter.2.cloned.1.call-start
  74.0 6.5 %multiply_convert_fusion = bf16[1536,768]{1,0:T(8,128)(2,1)} fusion(bf16[1536,1024]{1,0:T(8,128)(2,1)} %all-gather.2.cloned.1.call-done, bf16[768,1024]{1,0:T(8,128)(2,1)} %param.11), kind=kOutput, calls=%fused_computation | convolution fusion | flops 2418278400 | bytes 7077888 | tf_op jit(solution)/shard_map/dot_general | solution.py:32
  80.5 0.0 copy-start.1
  80.5 0.0 copy-start.2
  80.5 0.0 reduce-scatter.2.cloned.1.call-update
  80.5 1.0 copy-done.1
  81.5 0.2 copy.14
  81.7 0.9 constant_dynamic-slice_fusion
  82.6 0.8 copy.18
  84.1 1.2 copy.13
  85.3 0.0 copy-done.2
  85.3 76.9 %all-reduce.2.cloned.1.call-done = bf16[768,1024]{0,1:T(8,128)(2,1)} async-done(((bf16[768,1024]{0,1:T(8,128)(2,1)}), bf16[768,1024]{0,1:T(8,128)(2,1)}) %all-reduce.2.cloned.1.call-update) | async-done | bytes 1572880 | tf_op jit(solution)/shard_map/psum | solution.py:41
  162.2 2.5 fusion.10
  164.8 2.0 copy.15
  166.7 2.0 copy.16
  168.7 2.0 copy.17
  170.7 185.0 %reduce-scatter.2.cloned.1.call-done = bf16[128,768]{1,0:T(8,128)(2,1)} async-done(((bf16[1536,768]{1,0:T(8,128)(2,1)}), bf16[128,768]{1,0:T(8,128)(2,1)}) %reduce-scatter.2.cloned.1.call-update) | async-done | bytes 196624 | tf_op jit(solution)/shard_map/reduce_scatter | solution.py:37
  (1 shorter events, 0.0 us)
Async XLA Ops:
  7.2 61.0 %copy-start = (bf16[1536,768]{1,0:T(8,128)(2,1)S(1)}, bf16[1536,768]{1,0:T(8,128)(2,1)}, u32[]{:S(2)}) copy-start(bf16[1536,768]{1,0:T(8,128)(2,1)} %param.8) | copy-start | bytes 7077892
  7.2 60.9 %all-gather.2.cloned.1.call-start = ((), (), s32[]{:S(2)}) async-start(), calls=%async_computation.1 | async-start | bytes 3538944 | tf_op jit(solution)/shard_map/all_gather | solution.py:27
  9.6 152.6 %all-reduce.2.cloned.1.call-start = ((), (), s32[]{:S(2)}) async-start(), calls=%async_computation.3 | async-start | bytes 3145728 | tf_op jit(solution)/shard_map/psum | solution.py:41
  73.9 281.8 %reduce-scatter.2.cloned.1.call-start = ((), (), s32[]{:S(2)}) async-start(), calls=%async_computation.2 | async-start | bytes 2555904 | tf_op jit(solution)/shard_map/reduce_scatter | solution.py:37
  80.5 1.0 copy-start.1
  80.5 4.8 %copy-start.2 = (s32[1,96]{1,0:T(1,128)S(1)}, s32[1,96]{1,0:T(1,128)}, u32[]{:S(2)}) copy-start(s32[1,96]{1,0:T(1,128)} %param.15) | copy-start | bytes 1156
Sparse Core Ops, SparseCore 0:
  10.9 57.1 all-gather.1
  74.1 88.1 all-reduce.1
  168.2 187.4 reduce-scatter.1
where the time goes:
time: 363 us; the launch traced here: 362 us
  waiting for transfers between devices  320 us (88%)
  between operations  14.5 us (4%)
  matrix products  12.3 us (3%)
  local copies, waits for them, and re-layouts  10.1 us (3%)
  other arithmetic  4.91 us (1%)
    reduce_scatter x1, waiting for transfers between devices, body(): lax.psum_scatter(term_rows.astype(jnp.bfloat16), 'col', scatter_dimension...  185 us
    psum x1, waiting for transfers between devices, body(): summed = lax.psum(grad_acc.astype(jnp.bfloat16), 'dp').astype(jnp.float32)  76.9 us
    all_gather x1, waiting for transfers between devices, body(): portion = lax.all_gather(local_grad, 'row', axis=0, tiled=True)  58.4 us
    unnamed x12, local copies, waits for them, and re-layouts  9.14 us
  transfers between devices with their start and end apart: 3, of which 3 were waited for; matrix products, arithmetic and copies ran while one was open for 5% of the time, Pallas kernels for 0%

commit v1 on v0

v1 whole, which is shorter than its diff:
```python
import jax
import jax.numpy as jnp
from jax import lax
from jax.experimental import pallas as pl
from jax.experimental.pallas import tpu as pltpu
from jax.sharding import PartitionSpec as P

MESH = pl.DeviceIdType.MESH
D = 6144
learning_rate = 0.5
NZ = 4
NH = 3
NK = 2
STEPS = 7


def gelu_slope(values):
    normal_cdf = 0.5 * (1.0 + lax.erf(values * 0.7071067811865476))
    density = jnp.exp(-0.5 * values * values) * 0.3989422804014327
    return normal_cdf + values * density


def remote(src, dst, send_sem, recv_sem, device):
    return pltpu.make_async_remote_copy(
        src_ref=src, dst_ref=dst, send_sem=send_sem, recv_sem=recv_sem, device_id=device, device_id_type=MESH
    )


def kernel(
    inputs_hbm, pre_hbm, out_hbm, weight_hbm, share_ref, igrad_ref,
    inp, pre, outg, wgt, portion, acc, term, opp, xrecv, zsum, zrecv, ysend, yrecv,
    load_sem, zs, zr, cs, cr, opps, oppr, xs, xr, hs, hr, ys, yr,
):
    groups = lax.axis_size("dp")
    y = lax.axis_index("dp")
    row = lax.axis_index("row")
    col = lax.axis_index("col")
    zl, c = row // 2, row % 2
    x, zh = col // NH, col % NH
    multiplier = 1.0 / D**0.5
    token_block = pre.shape[0]
    half = token_block
    piece = token_block // NK
    shard = acc.shape[0] // groups
    cols = acc.shape[1] // 2

    partner = {"row": row + 1 - 2 * c}
    z_up, z_down = {"row": row + 2}, {"row": row - 2}
    x_up = {"col": (x + 1) % NZ * NH + zh}
    x_down = {"col": (x + NZ - 1) % NZ * NH + zh}
    h_peer = [{"col": x * NH + (zh + j) % NH} for j in (1, 2)]
    y_peer = [{"dp": (y + 1) % groups}, {"dp": (y + groups - 1) % groups}]

    barrier = pltpu.get_barrier_semaphore()
    greet = [
        partner, {"row": (row + 2) % (2 * NZ)}, {"row": (row + 2 * NZ - 2) % (2 * NZ)},
        x_up, x_down, *h_peer, *y_peer,
    ]
    for device in greet:
        pl.semaphore_signal(barrier, inc=1, device_id=device, device_id_type=MESH)

    loads = [
        pltpu.make_async_copy(pre_hbm, pre, load_sem.at[0]),
        pltpu.make_async_copy(out_hbm, outg, load_sem.at[1]),
        pltpu.make_async_copy(weight_hbm, wgt, load_sem.at[2]),
        pltpu.make_async_copy(inputs_hbm, inp, load_sem.at[3]),
    ]
    for load in loads:
        load.start()
    loads[0].wait()
    loads[1].wait()

    def z_copy(way, q, k):
        block = portion.at[q, c, k]
        return remote(block, block, zs.at[way, q, k], zr.at[q, k], z_up if way == 0 else z_down)

    def c_copy(q, k):
        block = portion.at[q, c, k]
        return remote(block, block, cs.at[q, k], cr.at[q, k], partner)

    def c_arrival(q, k):
        block = portion.at[q, 1 - c, k]
        return remote(block, block, cs.at[q, k], cr.at[q, k], partner)

    tile = 16

    def local_grad(k):
        def body(i, carry):
            start = pl.multiple_of(i * tile, tile)
            a = pre[pl.ds(pl.multiple_of(k * piece + start, tile), tile), :].astype(jnp.float32)
            g = outg[pl.ds(pl.multiple_of(k * piece + start, tile), tile), :].astype(jnp.float32)
            portion[zl, c, k, pl.ds(start, tile), :] = (g * gelu_slope(a)).astype(jnp.bfloat16)
            return carry

        lax.fori_loop(0, piece // tile, body, 0)

    for k in range(NK):
        local_grad(k)
        if k == 0:
            pl.semaphore_wait(barrier, len(greet))

        @pl.when(zl < NZ - 1)
        def _():
            z_copy(0, zl, k).start()

        @pl.when(zl > 0)
        def _():
            z_copy(1, zl, k).start()

        c_copy(zl, k).start()

    def zero(i, carry):
        acc[pl.ds(pl.multiple_of(i * 8, 8), 8), :] = jnp.zeros((8, acc.shape[1]), jnp.float32)
        return carry

    lax.fori_loop(0, acc.shape[0] // 8, zero, 0)
    loads[2].wait()
    loads[3].wait()

    def opp_copy(p, which):
        return remote(
            term.at[p, pl.ds(which * half, half)], opp.at[which], opps.at[which], oppr.at[which],
            x_down if which == 0 else x_up,
        )

    def x_copy(p, side, part):
        window = pl.ds(part * half, half)
        return remote(
            term.at[p, window], xrecv.at[side, window], xs.at[side, part], xr.at[side, part],
            x_down if side == 0 else x_up,
        )

    p_one = (x + NZ - 1) % NZ
    p_three = (x + 1) % NZ
    p_two = (x + 2) % NZ

    def absorb(p, which):
        opp_copy(p, which).wait_recv()
        base = which * half

        def body(i, carry):
            at = pl.multiple_of(base + i * 32, 32)
            own = term[p, pl.ds(at, 32), :].astype(jnp.float32)
            come = opp[which, pl.ds(pl.multiple_of(i * 32, 32), 32), :].astype(jnp.float32)
            term[p, pl.ds(at, 32), :] = (own + come).astype(jnp.bfloat16)
            return carry

        lax.fori_loop(0, half // 32, body, 0)
        x_copy(p, which, which).start()

    def h_copy(j):
        return remote(zsum.at[(zh + j) % NH], zrecv.at[j - 1], hs.at[j - 1], hr.at[j - 1], h_peer[j - 1])

    def collect():
        for side in range(2):
            for part in range(2):
                x_copy(x, side, part).wait_recv()
        for j in range(NH):

            def body(i, carry):
                at = pl.multiple_of(j * 128 + i * 32, 32)
                total = (
                    term[x, pl.ds(at, 32), :].astype(jnp.float32)
                    + xrecv[0, pl.ds(at, 32), :].astype(jnp.float32)
                    + xrecv[1, pl.ds(at, 32), :].astype(jnp.float32)
                )
                zsum[j, pl.ds(pl.multiple_of(i * 32, 32), 32), :] = total.astype(jnp.bfloat16)
                return carry

            lax.fori_loop(0, 128 // 32, body, 0)
        for j in (1, 2):
            h_copy(j).start()

    def later(d):
        @pl.when(jnp.abs(zl - p_one) == d - 1)
        def _():
            absorb(p_one, 0)

        @pl.when(jnp.abs(zl - p_three) == d - 1)
        def _():
            absorb(p_three, 1)

        @pl.when(jnp.abs(zl - x) == d - 2)
        def _():
            collect()

    def compute(q):
        for k in range(NK):
            c_arrival(q, k).wait_recv()
        tokens = portion[q].reshape(2 * token_block, portion.shape[-1])

        def product(n, carry):
            at = pl.ds(pl.multiple_of(n * 256, 256), 256)
            part = lax.dot_general(
                tokens, wgt[at, :], (((1,), (1,)), ((), ())), preferred_element_type=jnp.float32
            )
            term[q, :, at] = (part * multiplier).astype(jnp.bfloat16)
            return carry

        lax.fori_loop(0, wgt.shape[0] // 256, product, 0)

        @pl.when(p_two == q)
        def _():
            opp_copy(q, 0).start()
            opp_copy(q, 1).start()

        @pl.when(p_one == q)
        def _():
            x_copy(q, 0, 1).start()

        @pl.when(p_three == q)
        def _():
            x_copy(q, 1, 0).start()

        def outer(m, carry):
            at = pl.ds(pl.multiple_of(m * 256, 256), 256)
            acc[at, :] += lax.dot_general(
                inp[q, :, at], tokens, (((0,), (0,)), ((), ())), preferred_element_type=jnp.float32
            )
            return carry

        lax.fori_loop(0, acc.shape[0] // 256, outer, 0)

    def distance(d, carry):
        @pl.when(d > 0)
        def _():
            for k in range(NK):

                @pl.when(zl - d >= 0)
                def _():
                    q = zl - d
                    z_copy(0, q, k).wait_recv()

                    @pl.when(zl < NZ - 1)
                    def _():
                        z_copy(0, q, k).start()

                    c_copy(q, k).start()

                @pl.when(zl + d < NZ)
                def _():
                    q = zl + d
                    z_copy(1, q, k).wait_recv()

                    @pl.when(zl > 0)
                    def _():
                        z_copy(1, q, k).start()

                    c_copy(q, k).start()

        def side(j, carry):
            q = zl - d + 2 * d * j

            @pl.when((q >= 0) & (q < NZ))
            def _():
                compute(q)

            return carry

        lax.fori_loop(0, 1 + jnp.minimum(d, 1), side, 0)
        later(d)
        return carry

    lax.fori_loop(0, NZ, distance, 0)

    def y_copy(way, i):
        return remote(ysend.at[way, i], yrecv.at[way, i], ys.at[way, i], yr.at[way, i], y_peer[way])

    def y_step(i, absorbed):
        for way in range(2):
            k = groups // 2 - (i + 1) // 2
            target = (y + k) % groups if way == 0 else (y + groups - k) % groups
            which = (i + way) % 2
            rows = pl.ds(pl.multiple_of(target * shard, 8), shard)
            window = pl.ds(pl.multiple_of(which * cols, 128), cols)
            own = acc[rows, window]
            if absorbed:
                y_copy(way, i - 2).wait_recv()
                own = own + yrecv[way, i - 2].astype(jnp.float32)
            ysend[way, i] = own.astype(jnp.bfloat16)
            y_copy(way, i).start()

    y_step(0, False)
    y_step(1, False)

    def y_loop(i, carry):
        y_step(i, True)

        @pl.when(i == 4)
        def _():
            later(NZ)

        return carry

    lax.fori_loop(2, STEPS, y_loop, 0)
    later(NZ + 1)

    rows = pl.ds(pl.multiple_of(y * shard, 8), shard)
    for way in range(2):
        for i in (STEPS - 2, STEPS - 1):
            y_copy(way, i).wait_recv()
    share_ref[:, :cols] = (
        acc[rows, :cols] + yrecv[0, STEPS - 1].astype(jnp.float32) + yrecv[1, STEPS - 2].astype(jnp.float32)
    )
    share_ref[:, cols:] = (
        acc[rows, cols:] + yrecv[0, STEPS - 2].astype(jnp.float32) + yrecv[1, STEPS - 1].astype(jnp.float32)
    )
    for j in (1, 2):
        h_copy(j).wait_recv()
    igrad_ref[...] = (
        zsum[zh].astype(jnp.float32) + zrecv[0].astype(jnp.float32) + zrecv[1].astype(jnp.float32)
    )

    def drain(q, carry):
        for k in range(NK):
            c_copy(q, k).wait_send()

            @pl.when((q <= zl) & (zl < NZ - 1))
            def _():
                z_copy(0, q, k).wait_send()

            @pl.when((q >= zl) & (zl > 0))
            def _():
                z_copy(1, q, k).wait_send()

        return carry

    lax.fori_loop(0, NZ, drain, 0)
    for which in range(2):
        opp_copy(p_two, which).wait_send()
        x_copy(p_one, 0, which).wait_send()
        x_copy(p_three, 1, which).wait_send()
        h_copy(which + 1).wait_send()

    def y_drain(i, carry):
        y_copy(0, i).wait_send()
        y_copy(1, i).wait_send()
        return carry

    lax.fori_loop(0, STEPS, y_drain, 0)


def body(inputs, pre_act, out_grad, weight, swag_mean, swag_square, snapshots, update_flag):
    tokens, width = inputs.shape
    block, hidden = pre_act.shape
    groups = lax.axis_size("dp")
    shard = width // groups
    pair = 2 * block
    bf, f32 = jnp.bfloat16, jnp.float32
    dma = pltpu.SemaphoreType.DMA
    share, igrad = pl.pallas_call(
        kernel,
        out_shape=(
            jax.ShapeDtypeStruct((shard, hidden), f32),
            jax.ShapeDtypeStruct((pair // NH, width), f32),
        ),
        in_specs=[pl.BlockSpec(memory_space=pl.ANY)] * 4,
        out_specs=(pl.BlockSpec(memory_space=pltpu.VMEM), pl.BlockSpec(memory_space=pltpu.VMEM)),
        scratch_shapes=[
            pltpu.VMEM((NZ, pair, width), bf),
            pltpu.VMEM((block, hidden), bf),
            pltpu.VMEM((block, hidden), bf),
            pltpu.VMEM((width, hidden), bf),
            pltpu.VMEM((NZ, 2, NK, block // NK, hidden), bf),
            pltpu.VMEM((width, hidden), f32),
            pltpu.VMEM((NZ, pair, width), bf),
            pltpu.VMEM((2, block, width), bf),
            pltpu.VMEM((2, pair, width), bf),
            pltpu.VMEM((NH, pair // NH, width), bf),
            pltpu.VMEM((2, pair // NH, width), bf),
            pltpu.VMEM((2, STEPS, shard, hidden // 2), bf),
            pltpu.VMEM((2, STEPS, shard, hidden // 2), bf),
            dma((4,)),
            dma((2, NZ, NK)), dma((NZ, NK)), dma((NZ, NK)), dma((NZ, NK)),
            dma((2,)), dma((2,)), dma((2, 2)), dma((2, 2)), dma((2,)), dma((2,)),
            dma((2, STEPS)), dma((2, STEPS)),
        ],
        compiler_params=pltpu.CompilerParams(collective_id=0, has_side_effects=True),
    )(inputs.reshape(NZ, pair, width), pre_act, out_grad, weight)

    replica_index = lax.axis_index("dp")
    own_rows = lax.dynamic_slice_in_dim(weight, replica_index * shard, shard, 0).astype(f32)
    stepped = own_rows - learning_rate * (share / (tokens * groups) ** 0.5)
    blend = update_flag[0].astype(f32)[:, None] / (snapshots[0].astype(f32) + 1.0)
    mean_new = swag_mean[0] + blend * (stepped - swag_mean[0])
    square_new = swag_square[0] + blend * (stepped * stepped - swag_square[0])
    return (igrad.astype(bf), stepped[None], mean_new[None], square_new[None])


def solution(mesh):
    in_specs = (
        P("dp", "row"),
        P(("dp", "row"), "col"),
        P(("dp", "row"), "col"),
        P("row", "col"),
        P("dp", "row", "col"),
        P("dp", "row", "col"),
        P(),
        P("dp", "row"),
    )
    out_specs = (
        P(("dp", "col"), "row"),
        P("dp", "row", "col"),
        P("dp", "row", "col"),
        P("dp", "row", "col"),
    )
    return jax.shard_map(body, mesh=mesh, in_specs=in_specs, out_specs=out_specs, check_vma=False)
```

time: 363 us -> 79.6 us (0.22)
  waiting for transfers between devices: 320 us -> 0 us
  Pallas kernels: 0 us -> 73.5 us
  between operations: 14.5 us -> 1.29 us
  matrix products: 12.3 us -> 0 us
  local copies, waits for them, and re-layouts: 10.1 us -> 0.01 us
    reduce_scatter x1 -> x0, waiting for transfers between devices: 185 us -> none  [body(): lax.psum_scatter(term_rows.astype(jnp.bfloat16), 'col', scatter_dimension...]
    psum x1 -> x0, waiting for transfers between devices: 76.9 us -> none  [body(): summed = lax.psum(grad_acc.astype(jnp.bfloat16), 'dp').astype(jnp.float32)]
    pallas_call x0 -> x1, Pallas kernels: none -> 73.5 us  [body(): pl.pallas_call(kernel, out_shape=(jax.ShapeDtypeStruct((shard, hidden), f...]
    all_gather x1 -> x0, waiting for transfers between devices: 58.4 us -> none  [body(): portion = lax.all_gather(local_grad, 'row', axis=0, tiled=True)]
    dot_general x2 -> x0, matrix products: 12.3 us -> none  [the longest x1 6.47 us: body(): lax.dot_general(portion, weight, (((1,), (1,)), ((), ())), preferred_elem...]
    unnamed x12 -> x4, local copies, waits for them, and re-layouts: 9.14 us -> 0.01 us
  transfers between devices with their start and end apart: 3 -> 0, of which waited for: 3 -> 0; matrix products, arithmetic and copies ran while one was open for 5% -> 0% of each run, Pallas kernels for 0% -> 0%
where the time goes in v1:
time: 79.6 us; the launch traced here: 79.4 us
  Pallas kernels  73.5 us (92%)
  other arithmetic  4.61 us (6%)
  between operations  1.29 us (2%)
    pallas_call x1, Pallas kernels, body(): pl.pallas_call(kernel, out_shape=(jax.ShapeDtypeStruct((shard, hidden), f...  73.5 us
    broadcast_in_dim x1, other arithmetic, body(): return (igrad.astype(bf), stepped[None], mean_new[None], square_new[None])  2.26 us
    convert_element_type x1, other arithmetic, body(): return (igrad.astype(bf), stepped[None], mean_new[None], square_new[None])  1.69 us

profile of v1, /device:TPU:6, one launch (start us, length us, event | category | flops | bytes accessed | tf_op | source)
XLA Modules:
  0.0 79.4 jit_solution(15934105134487191254)
XLA Ops:
  1.3 0.7 divide_bitcast_fusion
  1.9 0.0 copy-start
  1.9 0.0 copy-start.1
  1.9 73.5 %shard_map.111 = (f32[96,1024]{1,0:T(8,128)}, f32[128,768]{1,0:T(8,128)}) custom-call(bf16[4,384,768]{2,1,0:T(8,128)(2,1)} %bitcast.28, bf16[192,1024]{1,0:T(8,128)(2,1)} %pre_hbm.1, bf16[192,1024]{1,0:T(8,128)(2,1)} %out_hbm.1, bf16[768,1024]{1,0:T(8,128)(2,1)} %weight_hbm.1), custom_call_target="tpu_custom_call" | custom-call | tf_op jit(solution)/shard_map/pallas_call | solution.py:351
  75.5 1.7 %convert_element_type.18 = bf16[128,768]{1,0:T(8,128)(2,1)} convert(f32[128,768]{1,0:T(8,128)} %get-tuple-element.6) | non-fusion elementwise | flops 98304 | bytes 589824 | tf_op jit(solution)/shard_map/convert_element_type | solution.py:387
  77.2 0.0 copy-done
  77.2 0.0 copy-done.1
  77.2 2.3 %fusion.1 = (f32[1,96,1024]{2,1,0:T(8,128)}, f32[1,96,1024]{2,1,0:T(8,128)}, f32[1,96,1024]{2,1,0:T(8,128)}) fusion(f32[1,96,1024]{2,1,0:T(8,128)S(1)} %copy-done, f32[96]{0:T(128)S(1)} %divide_bitcast_fusion, f32[96,1024]{1,0:T(8,128)} %get-tuple-element.7, bf16[768,1024]{1,0:T(8,128)(2,1)} %weight_hbm.1, s32[]{:T(128)S(6)} %select_n.3, ...), kind=kLoop, calls=%fused_computation.3 | loop fusion | flops 983040 | bytes 2556292 | tf_op jit(solution)/shard_map/broadcast_in_dim | solution.py:387
Async XLA Ops:
  1.9 75.2 %copy-start = (f32[1,96,1024]{2,1,0:T(8,128)S(1)}, f32[1,96,1024]{2,1,0:T(8,128)}, u32[]{:S(2)}) copy-start(f32[1,96,1024]{2,1,0:T(8,128)} %param.13) | copy-start | bytes 1179652
  1.9 75.2 %copy-start.1 = (f32[1,96,1024]{2,1,0:T(8,128)S(1)}, f32[1,96,1024]{2,1,0:T(8,128)}, u32[]{:S(2)}) copy-start(f32[1,96,1024]{2,1,0:T(8,128)} %param.12) | copy-start | bytes 1179652

commit v2 on v1

v2 whole, which is shorter than its diff:
```python
import jax
import jax.numpy as jnp
from jax import lax
from jax.experimental import pallas as pl
from jax.experimental.pallas import tpu as pltpu
from jax.sharding import PartitionSpec as P

MESH = pl.DeviceIdType.MESH
D = 6144
learning_rate = 0.5
NZ = 4
NH = 3
NK = 2
STEPS = 7
ABSORB, COLLECT = 1, 3
HOLD = 0
TAIL = {1: 0, 3: 1, 4: 2}
REACH = NZ * (NH - 1)
PER = 6


def gelu_slope(values):
    normal_cdf = 0.5 * (1.0 + lax.erf(values * 0.7071067811865476))
    density = jnp.exp(-0.5 * values * values) * 0.3989422804014327
    return normal_cdf + values * density


def remote(src, dst, send_sem, recv_sem, device):
    return pltpu.make_async_remote_copy(
        src_ref=src, dst_ref=dst, send_sem=send_sem, recv_sem=recv_sem, device_id=device, device_id_type=MESH
    )


def send_orders():
    orders, starts, extras = [], [], []
    arriving = []
    for z in range(NZ):
        own = [(z, k) for k in range(NK)]
        first = NK if z == 0 else min(NK, 2 if z == NZ - 2 else 1)
        start, rest = own[:first], own[first:]
        order, extra = list(start), []
        for piece in arriving:
            order.append(piece)
            if rest:
                extra.append(rest[0][1])
                order.append(rest.pop(0))
            else:
                extra.append(-1)
        order += rest
        orders.append(order)
        starts.append(first)
        extras.append(extra)
        arriving = order
    return orders, starts, extras


def packed(entries, length):
    words = []
    for line in entries:
        line = list(line) + [-1] * (length - len(line))
        line = [e + 1 for e in line]
        words.append([
            sum(e << (5 * i) for i, e in enumerate(line[w : w + PER])) for w in range(0, length, PER)
        ])
    return words


def choose(words, zl):
    out = []
    for w in range(len(words[0])):
        value = jnp.int32(words[0][w])
        for v in range(1, NZ):
            value = jnp.where(zl == v, jnp.int32(words[v][w]), value)
        out.append(value)
    return out


def look(words, s):
    value = jnp.int32(0)
    for w, word in enumerate(words):
        value = jnp.where((s >= PER * w) & (s < PER * (w + 1)), word, value)
    return ((value >> (5 * ((s + PER) % PER))) & 31) - 1


def kernel(
    inputs_hbm, pre_hbm, out_hbm, weight_hbm, snap_hbm, flag_hbm, step_ref, igrad_ref, blend_ref,
    snap, flag, inp, pre, outg, wgt, portion, acc, term, opp, xrecv, zsum, zrecv, ysend, yrecv,
    load_sem, zs, zr, cs, cr, opps, oppr, xs, xr, hs, hr, ys, yr, token,
):
    groups = lax.axis_size("dp")
    y = lax.axis_index("dp")
    row = lax.axis_index("row")
    col = lax.axis_index("col")
    zl, c = row // 2, row % 2
    x, zh = col // NH, col % NH
    multiplier = 1.0 / D**0.5
    token_block = pre.shape[0]
    piece = token_block // NK
    hidden = portion.shape[-1]
    shard = acc.shape[0] // groups
    cols = acc.shape[1] // 2
    third = 2 * token_block // NH
    last = NZ * NK

    partner = {"row": row + 1 - 2 * c}
    z_up, z_down = {"row": row + 2}, {"row": row - 2}
    x_up = {"col": (x + 1) % NZ * NH + zh}
    x_down = {"col": (x + NZ - 1) % NZ * NH + zh}
    y_peer = [{"dp": (y + 1) % groups}, {"dp": (y + groups - 1) % groups}]

    barrier = pltpu.get_barrier_semaphore()
    greet = [partner, x_up, x_down, *y_peer]
    for device in greet:
        pl.semaphore_signal(barrier, inc=1, device_id=device, device_id_type=MESH)
    chain = NZ * NH - 1
    place = zh * NZ + zl
    line_up = {"row": (row + 2) % (2 * NZ), "col": (col + (zl + 1) // NZ) % (NZ * NH)}
    line_down = {"row": (row + 2 * NZ - 2) % (2 * NZ), "col": (col + NZ * NH - (NZ - zl) // NZ) % (NZ * NH)}

    @pl.when(place < chain)
    def _():
        pl.semaphore_signal(barrier, inc=1, device_id=line_up, device_id_type=MESH)

    @pl.when(place > 0)
    def _():
        pl.semaphore_signal(barrier, inc=1, device_id=line_down, device_id_type=MESH)

    arrivals = len(greet) + jnp.minimum(place, 1) + jnp.minimum(chain - place, 1)

    def hear(n):
        for way, there, onward, device in (
            (0, place - n >= 0, place < chain, line_up), (1, place + n <= chain, place > 0, line_down),
        ):

            @pl.when((n >= 2) & (n <= REACH) & there)
            def _():
                pl.semaphore_wait(token.at[way], 1)

            @pl.when((n < REACH) & there & onward)
            def _():
                pl.semaphore_signal(token.at[way], inc=1, device_id=device, device_id_type=MESH)

    loads = [
        pltpu.make_async_copy(pre_hbm, pre, load_sem.at[0]),
        pltpu.make_async_copy(out_hbm, outg, load_sem.at[1]),
        pltpu.make_async_copy(weight_hbm, wgt, load_sem.at[2]),
        pltpu.make_async_copy(snap_hbm, snap, load_sem.at[3]),
        pltpu.make_async_copy(flag_hbm, flag, load_sem.at[4]),
        *(
            pltpu.make_async_copy(inputs_hbm.at[q, h], inp.at[q, :, h], load_sem.at[5 + 2 * q + h])
            for q in range(NZ)
            for h in range(2)
        ),
    ]
    for load in loads:
        load.start()

    orders, starts, extras = send_orders()
    code = lambda line: [q * NK + k for q, k in line]
    flip = lambda line: [(NZ - 1 - q, k) for q, k in line]
    own_steps = [[(z, k) for k in range(NK)] for z in range(NZ)]
    none = [-1] * NK
    below = [code(own_steps[z]) + (code(orders[z - 1]) if z > 0 else []) for z in range(NZ)]
    above = [none + (code(flip(orders[NZ - 2 - z])) if z < NZ - 1 else []) for z in range(NZ)]
    more_up = [none + extras[z] for z in range(NZ)]
    more_down = [none + extras[NZ - 1 - z] for z in range(NZ)]
    start_up = choose([[starts[z]] for z in range(NZ)], zl)[0]
    start_down = choose([[starts[NZ - 1 - z]] for z in range(NZ)], zl)[0]
    below, above, more_up, more_down = (
        choose(packed(t, last), zl) for t in (below, above, more_up, more_down)
    )

    def z_copy(way, q, k):
        block = portion.at[q, k, c]
        return remote(block, block, zs.at[way, q, k], zr.at[q, k], z_up if way == 0 else z_down)

    def c_copy(q, k):
        block = portion.at[q, k, c]
        return remote(block, block, cs.at[q, k], cr.at[q, k], partner)

    def c_arrival(q, k):
        block = portion.at[q, k, 1 - c]
        return remote(block, block, cs.at[q, k], cr.at[q, k], partner)

    tile = 16

    def local_grad(k):
        def body(i, carry):
            start = pl.multiple_of(i * tile, tile)
            a = pre[pl.ds(pl.multiple_of(k * piece + start, tile), tile), :].astype(jnp.float32)
            g = outg[pl.ds(pl.multiple_of(k * piece + start, tile), tile), :].astype(jnp.float32)
            portion[zl, k, c, pl.ds(start, tile), :] = (g * gelu_slope(a)).astype(jnp.bfloat16)
            return carry

        lax.fori_loop(0, piece // tile, body, 0)

    loads[0].wait()
    loads[1].wait()
    for k in range(NK):
        local_grad(k)
        if k == 0:
            pl.semaphore_wait(barrier, arrivals)

        @pl.when((zl < NZ - 1) & (k < start_up))
        def _():
            z_copy(0, zl, k).start()

        @pl.when((zl > 0) & (k < start_down))
        def _():
            z_copy(1, zl, k).start()

        c_copy(zl, k).start()

    def zero(i, carry):
        acc[pl.ds(pl.multiple_of(i * 8, 8), 8), :] = jnp.zeros((8, acc.shape[1]), jnp.float32)
        return carry

    lax.fori_loop(0, acc.shape[0] // 8, zero, 0)
    for load in loads[2:]:
        load.wait()
    flags = jnp.broadcast_to(flag[...].astype(jnp.float32), (shard, shard))
    here = lax.broadcasted_iota(jnp.int32, (shard, shard), 0) == lax.broadcasted_iota(jnp.int32, (shard, shard), 1)
    column = jnp.sum(jnp.where(here, flags, 0.0), axis=1, keepdims=True)
    blend_ref[...] = jnp.broadcast_to(column / (snap[0].astype(jnp.float32) + 1.0), blend_ref.shape)

    def opp_copy(p, k, which):
        return remote(
            term.at[p, which, k], opp.at[which, k], opps.at[which, k], oppr.at[which, k],
            x_down if which == 0 else x_up,
        )

    def x_copy(p, k, side, part):
        return remote(
            term.at[p, part, k], xrecv.at[side, part, k], xs.at[side, part, k], xr.at[side, part, k],
            x_down if side == 0 else x_up,
        )

    def absorb(p, k, which):
        opp_copy(p, k, which).wait_recv()

        def body(i, carry):
            at = pl.ds(pl.multiple_of(i * 48, 16), 48)
            own = term[p, which, k, at, :].astype(jnp.float32)
            come = opp[which, k, at, :].astype(jnp.float32)
            term[p, which, k, at, :] = (own + come).astype(jnp.bfloat16)
            return carry

        lax.fori_loop(0, piece // 48, body, 0)
        x_copy(p, k, which, which).start()

    spans = []
    for k in range(NK):
        found = []
        for t in range(NH):
            for h in range(2):
                lo = max(t * third, h * token_block + k * piece)
                hi = min((t + 1) * third, h * token_block + (k + 1) * piece)
                if hi > lo:
                    found.append((t, lo, hi - lo))
        assert len({t for t, _, _ in found}) == len(found)
        spans.append(found)

    def h_copy(k, t, lo, size):
        return remote(
            zsum.at[pl.ds(lo, size)], zrecv.at[zh, pl.ds(lo - t * third, size)], hs.at[k, t], hr.at[k, zh],
            {"col": x * NH + t},
        )

    def h_arrival(k, source, lo, size):
        t = lo // third
        return remote(
            zsum.at[pl.ds(lo, size)], zrecv.at[source, pl.ds(lo - t * third, size)], hs.at[k, t],
            hr.at[k, source], {"col": x * NH + source},
        )

    def h_send(k):
        for kk in range(NK):

            @pl.when(k == kk)
            def _():
                for t, lo, size in spans[kk]:

                    @pl.when(zh != t)
                    def _():
                        h_copy(kk, t, lo, size).start()

    def collect(k, send):
        for part in range(2):
            for side in range(2):
                x_copy(x, k, side, part).wait_recv()

            def body(i, carry):
                at = pl.ds(pl.multiple_of(i * 48, 16), 48)
                total = (
                    term[x, part, k, at, :].astype(jnp.float32)
                    + xrecv[0, part, k, at, :].astype(jnp.float32)
                    + xrecv[1, part, k, at, :].astype(jnp.float32)
                )
                to = pl.ds(pl.multiple_of(part * token_block + k * piece + i * 48, 16), 48)
                zsum[to, :] = total.astype(jnp.bfloat16)
                return carry

            lax.fori_loop(0, piece // 48, body, 0)
        if send is True:
            h_send(k)
        else:

            @pl.when(send)
            def _():
                h_send(k)

    def events(s):
        return (look(below, s), look(above, s))

    def duty(s, send):
        for e in events(s - ABSORB):
            p, k = e // NK, e % NK

            @pl.when((e >= 0) & ((x + NZ - p) % NZ == 1))
            def _():
                absorb(p, k, 0)

            @pl.when((e >= 0) & ((x + NZ - p) % NZ == 3))
            def _():
                absorb(p, k, 1)

        for e in events(s - COLLECT):
            p, k = e // NK, e % NK

            @pl.when((e >= 0) & (p == x))
            def _():
                collect(k, send)

    def product(q, k):
        c_arrival(q, k).wait_recv()
        tokens = portion[q, k].reshape(2 * piece, hidden)
        part = lax.dot_general(
            tokens, wgt[...], (((1,), (1,)), ((), ())), preferred_element_type=jnp.float32
        )
        term[q, :, k] = (part * multiplier).astype(jnp.bfloat16).reshape(2, piece, wgt.shape[0])
        rel = (x + NZ - q) % NZ

        @pl.when(rel == 2)
        def _():
            opp_copy(q, k, 0).start()
            opp_copy(q, k, 1).start()

        @pl.when(rel == 1)
        def _():
            x_copy(q, k, 0, 1).start()

        @pl.when(rel == 3)
        def _():
            x_copy(q, k, 1, 0).start()

    def outer(q, k):
        both = pl.ds(k + 1 - NK // 2, NK // 2)
        tokens = portion[q, both].reshape(token_block, hidden)
        acc[...] += lax.dot_general(
            inp[q, both].reshape(token_block, acc.shape[0]), tokens, (((0,), (0,)), ((), ())),
            preferred_element_type=jnp.float32,
        )

    def deferred(s, carry):
        for e in events(s):

            @pl.when((e >= 0) & (e // NK == x))
            def _():
                h_send(e % NK)

        return carry

    def step(s, carry):
        hear(s + 1)
        pair = events(s)

        @pl.when(s >= NK)
        def _():
            for way, e, more in ((0, pair[0], more_up), (1, pair[1], more_down)):
                q, k = e // NK, e % NK
                onward = zl < NZ - 1 if way == 0 else zl > 0

                @pl.when(e >= 0)
                def _():
                    z_copy(way, q, k).wait_recv()

                    @pl.when(onward)
                    def _():
                        z_copy(way, q, k).start()

                    c_copy(q, k).start()
                    own = look(more, s)

                    @pl.when((own >= 0) & onward)
                    def _():
                        z_copy(way, zl, own).start()

        def products(j, carry):
            e = jnp.where(j == 0, pair[0], pair[1])

            @pl.when(e >= 0)
            def _():
                product(e // NK, e % NK)

            return carry

        def outers(j, carry):
            e = jnp.where(j == 0, pair[0], pair[1])

            @pl.when((e >= 0) & ((e + 1) % (NK // 2) == 0))
            def _():
                outer(e // NK, e % NK)

            return carry

        lax.fori_loop(0, 2, products, 0)
        duty(s, s < 0)
        lax.fori_loop(0, 2, outers, 0)
        return carry

    lax.fori_loop(0, last, step, 0)

    outside = (zl == 0) | (zl == NZ - 1)

    @pl.when(outside)
    def _():
        lax.fori_loop(0, last - COLLECT, deferred, 0)

    def y_copy(way, i):
        return remote(ysend.at[way, i], yrecv.at[way, i], ys.at[way, i], yr.at[way, i], y_peer[way])

    def y_step(i, carry):
        for way in range(2):
            k = groups // 2 - (i + 1) // 2
            target = (y + k) % groups if way == 0 else (y + groups - k) % groups
            which = (i + way) % 2
            rows = pl.ds(pl.multiple_of(target * shard, 8), shard)
            window = pl.ds(pl.multiple_of(which * cols, 128), cols)

            @pl.when(i < 2)
            def _():
                ysend[way, i] = acc[rows, window].astype(jnp.bfloat16)

            @pl.when(i >= 2)
            def _():
                y_copy(way, i - 2).wait_recv()
                ysend[way, i] = (acc[rows, window] + yrecv[way, i - 2].astype(jnp.float32)).astype(jnp.bfloat16)

            y_copy(way, i).start()

        go = jnp.int32(-1)
        for at, after in TAIL.items():
            go = jnp.where(i == at, after, go)

        @pl.when((i == HOLD) & jnp.logical_not(outside))
        def _():
            lax.fori_loop(0, last - COLLECT + sum(at < HOLD for at in TAIL), deferred, 0)

        @pl.when(go >= 0)
        def _():
            duty(last + go, outside | (i >= HOLD))

        return carry

    lax.fori_loop(0, STEPS, y_step, 0)

    rows = pl.ds(pl.multiple_of(y * shard, 16), shard)
    for way in range(2):
        for i in (STEPS - 2, STEPS - 1):
            y_copy(way, i).wait_recv()
    total_tokens = (NZ * 2 * token_block) * groups
    for window, up, down in (
        (slice(0, cols), STEPS - 1, STEPS - 2),
        (slice(cols, 2 * cols), STEPS - 2, STEPS - 1),
    ):
        share = acc[rows, window] + yrecv[0, up].astype(jnp.float32) + yrecv[1, down].astype(jnp.float32)
        step_ref[:, window] = wgt[rows, window].astype(jnp.float32) - learning_rate * (share / total_tokens**0.5)

    for t in range(NH):

        @pl.when(zh == t)
        def _():
            for source in range(NH):
                if source != t:
                    for k in range(NK):
                        for owner, lo, size in spans[k]:
                            if owner == t:
                                h_arrival(k, source, lo, size).wait_recv()
            others = [source for source in range(NH) if source != t]
            igrad_ref[...] = (
                zsum[pl.ds(t * third, third), :].astype(jnp.float32)
                + zrecv[others[0]].astype(jnp.float32)
                + zrecv[others[1]].astype(jnp.float32)
            ).astype(jnp.bfloat16)

    def drain(q, carry):
        for k in range(NK):
            c_copy(q, k).wait_send()

            @pl.when((q <= zl) & (zl < NZ - 1))
            def _():
                z_copy(0, q, k).wait_send()

            @pl.when((q >= zl) & (zl > 0))
            def _():
                z_copy(1, q, k).wait_send()

        return carry

    lax.fori_loop(0, NZ, drain, 0)
    for k in range(NK):
        for which in range(2):
            opp_copy((x + 2) % NZ, k, which).wait_send()
            x_copy((x + NZ - 1) % NZ, k, 0, which).wait_send()
            x_copy((x + 1) % NZ, k, 1, which).wait_send()
        for t, lo, size in spans[k]:

            @pl.when(zh != t)
            def _():
                h_copy(k, t, lo, size).wait_send()

    def y_drain(i, carry):
        y_copy(0, i).wait_send()
        y_copy(1, i).wait_send()
        return carry

    lax.fori_loop(0, STEPS, y_drain, 0)


def finish(step_ref, igrad_ref, blend_ref, mean_ref, square_ref, igrad_out, step_out, mean_out, square_out):
    igrad_out[...] = igrad_ref[...]
    blend = blend_ref[:, :1]
    stepped = step_ref[...]
    step_out[0] = stepped
    mean_old, square_old = mean_ref[0], square_ref[0]
    mean_out[0] = mean_old + blend * (stepped - mean_old)
    square_out[0] = square_old + blend * (stepped * stepped - square_old)


def body(inputs, pre_act, out_grad, weight, swag_mean, swag_square, snapshots, update_flag):
    tokens, width = inputs.shape
    block, hidden = pre_act.shape
    groups = lax.axis_size("dp")
    shard = width // groups
    piece = block // NK
    third = 2 * block // NH
    bf, f32 = jnp.bfloat16, jnp.float32
    dma = pltpu.SemaphoreType.DMA
    vmem = pl.BlockSpec(memory_space=pltpu.VMEM)
    stepped, igrad, blend = pl.pallas_call(
        kernel,
        out_shape=(
            jax.ShapeDtypeStruct((shard, hidden), f32),
            jax.ShapeDtypeStruct((third, width), bf),
            jax.ShapeDtypeStruct((shard, 128), f32),
        ),
        in_specs=[pl.BlockSpec(memory_space=pl.ANY)] * 6,
        out_specs=(vmem, vmem, vmem),
        scratch_shapes=[
            pltpu.SMEM((1,), jnp.int32),
            pltpu.VMEM((1, shard), jnp.int32),
            pltpu.VMEM((NZ, NK, 2, piece, width), bf),
            pltpu.VMEM((block, hidden), bf),
            pltpu.VMEM((block, hidden), bf),
            pltpu.VMEM((width, hidden), bf),
            pltpu.VMEM((NZ, NK, 2, piece, hidden), bf),
            pltpu.VMEM((width, hidden), f32),
            pltpu.VMEM((NZ, 2, NK, piece, width), bf),
            pltpu.VMEM((2, NK, piece, width), bf),
            pltpu.VMEM((2, 2, NK, piece, width), bf),
            pltpu.VMEM((2 * block, width), bf),
            pltpu.VMEM((NH, third, width), bf),
            pltpu.VMEM((2, STEPS, shard, hidden // 2), bf),
            pltpu.VMEM((2, STEPS, shard, hidden // 2), bf),
            dma((5 + 2 * NZ,)),
            dma((2, NZ, NK)), dma((NZ, NK)), dma((NZ, NK)), dma((NZ, NK)),
            dma((2, NK)), dma((2, NK)), dma((2, 2, NK)), dma((2, 2, NK)), dma((NK, NH)), dma((NK, NH)),
            dma((2, STEPS)), dma((2, STEPS)),
            pltpu.SemaphoreType.REGULAR((2,)),
        ],
        compiler_params=pltpu.CompilerParams(collective_id=0, has_side_effects=True),
    )(inputs.reshape(NZ, 2, NK, piece, width), pre_act, out_grad, weight, snapshots, update_flag)

    moments = jax.ShapeDtypeStruct(swag_mean.shape, f32)
    return pl.pallas_call(
        finish,
        out_shape=(jax.ShapeDtypeStruct(igrad.shape, bf), moments, moments, moments),
        in_specs=[vmem] * 5,
        out_specs=(vmem, vmem, vmem, vmem),
    )(stepped, igrad, blend, swag_mean, swag_square)


def solution(mesh):
    in_specs = (
        P("dp", "row"),
        P(("dp", "row"), "col"),
        P(("dp", "row"), "col"),
        P("row", "col"),
        P("dp", "row", "col"),
        P("dp", "row", "col"),
        P(),
        P("dp", "row"),
    )
    out_specs = (
        P(("dp", "col"), "row"),
        P("dp", "row", "col"),
        P("dp", "row", "col"),
        P("dp", "row", "col"),
    )
    return jax.shard_map(body, mesh=mesh, in_specs=in_specs, out_specs=out_specs, check_vma=False)
```

time: 79.6 us -> 74 us (0.930)
  the two profiles are of different devices: /device:TPU:6 before, /device:TPU:31 now
where the time goes in v2:
time: 74 us; the launch traced here: 73.8 us
  Pallas kernels  72.6 us (98%)
  between operations  1.29 us (2%)
    pallas_call x1, Pallas kernels, body(): pl.pallas_call(kernel, out_shape=(jax.ShapeDtypeStruct((shard, hidden), f...  70 us
    pallas_call x1, Pallas kernels, body(): pl.pallas_call(finish, out_shape=(jax.ShapeDtypeStruct(igrad.shape, bf),...  2.52 us

profile of v2, /device:TPU:31, one launch (start us, length us, event | category | flops | bytes accessed | tf_op | source)
XLA Modules:
  0.0 73.8 jit_solution(17298001082394219539)
XLA Ops:
  1.3 70.0 %shard_map.111 = (f32[96,1024]{1,0:T(8,128)}, bf16[128,768]{1,0:T(8,128)(2,1)}, f32[96,128]{1,0:T(8,128)}) custom-call(bf16[4,2,2,96,768]{4,3,2,1,0:T(8,128)(2,1)} %bitcast.1, bf16[192,1024]{1,0:T(8,128)(2,1)} %pre_hbm.1, bf16[192,1024]{1,0:T(8,128)(2,1)} %out_hbm.1, bf16[768,1024]{1,0:T(8,128)(2,1)} %weight_hbm.1, s32[1]{0:T(128)S(6)} %copy.12.snap_hbm, ...), custom_call_target="tpu_custom_call" | custom-call | tf_op jit(solution)/shard_map/pallas_call | solution.py:550
  71.3 2.5 %shard_map.112 = (bf16[128,768]{1,0:T(8,128)(2,1)}, f32[1,96,1024]{2,1,0:T(8,128)}, f32[1,96,1024]{2,1,0:T(8,128)}, f32[1,96,1024]{2,1,0:T(8,128)}) custom-call(f32[96,1024]{1,0:T(8,128)} %get-tuple-element.7.step_ref, bf16[128,768]{1,0:T(8,128)(2,1)} %get-tuple-element.8.igrad_ref, f32[96,128]{1,0:T(8,128)} %get-tuple-element.9.blend_ref, ...), custom_call_target="tpu_custom_call" | custom-call | tf_op jit(solution)/shard_map/pallas_call | solution.py:585

commit v3 on v2

--- a/solution.py
+++ b/solution.py
@@ -13,7 +13,7 @@
 NK = 2
 STEPS = 7
 ABSORB, COLLECT = 1, 3
-HOLD = 0
+HOLD = (3, 1, -1)
 TAIL = {1: 0, 3: 1, 4: 2}
 REACH = NZ * (NH - 1)
 PER = 6
@@ -420,9 +420,9 @@
 
     lax.fori_loop(0, last, step, 0)
 
-    outside = (zl == 0) | (zl == NZ - 1)
-
-    @pl.when(outside)
+    hold = jnp.where(zh == 0, HOLD[0], jnp.where(zh == 1, HOLD[1], HOLD[2]))
+
+    @pl.when(hold < 0)
     def _():
         lax.fori_loop(0, last - COLLECT, deferred, 0)
 
@@ -452,13 +452,14 @@
         for at, after in TAIL.items():
             go = jnp.where(i == at, after, go)
 
-        @pl.when((i == HOLD) & jnp.logical_not(outside))
-        def _():
-            lax.fori_loop(0, last - COLLECT + sum(at < HOLD for at in TAIL), deferred, 0)
+        @pl.when(i == hold)
+        def _():
+            done = sum(jnp.where(at < hold, 1, 0) for at in TAIL)
+            lax.fori_loop(0, last - COLLECT + done, deferred, 0)
 
         @pl.when(go >= 0)
         def _():
-            duty(last + go, outside | (i >= HOLD))
+            duty(last + go, i >= hold)
 
         return carry
 

time: 74 us -> 72.3 us (0.977)
  the two profiles are of different devices: /device:TPU:31 before, /device:TPU:6 now
where the time goes in v3:
time: 72.3 us; the launch traced here: 72.1 us
  Pallas kernels  70.9 us (98%)
  between operations  1.29 us (2%)
    pallas_call x1, Pallas kernels, body(): pl.pallas_call(kernel, out_shape=(jax.ShapeDtypeStruct((shard, hidden), f...  68.3 us
    pallas_call x1, Pallas kernels, body(): pl.pallas_call(finish, out_shape=(jax.ShapeDtypeStruct(igrad.shape, bf),...  2.52 us

profile of v3, /device:TPU:6, one launch (start us, length us, event | category | flops | bytes accessed | tf_op | source)
XLA Modules:
  0.0 72.1 jit_solution(15114445580321024535)
XLA Ops:
  1.3 68.3 %shard_map.111 = (f32[96,1024]{1,0:T(8,128)}, bf16[128,768]{1,0:T(8,128)(2,1)}, f32[96,128]{1,0:T(8,128)}) custom-call(bf16[4,2,2,96,768]{4,3,2,1,0:T(8,128)(2,1)} %bitcast.1, bf16[192,1024]{1,0:T(8,128)(2,1)} %pre_hbm.1, bf16[192,1024]{1,0:T(8,128)(2,1)} %out_hbm.1, bf16[768,1024]{1,0:T(8,128)(2,1)} %weight_hbm.1, s32[1]{0:T(128)S(6)} %copy.12.snap_hbm, ...), custom_call_target="tpu_custom_call" | custom-call | tf_op jit(solution)/shard_map/pallas_call | solution.py:551
  69.6 2.5 %shard_map.112 = (bf16[128,768]{1,0:T(8,128)(2,1)}, f32[1,96,1024]{2,1,0:T(8,128)}, f32[1,96,1024]{2,1,0:T(8,128)}, f32[1,96,1024]{2,1,0:T(8,128)}) custom-call(f32[96,1024]{1,0:T(8,128)} %get-tuple-element.7.step_ref, bf16[128,768]{1,0:T(8,128)(2,1)} %get-tuple-element.8.igrad_ref, f32[96,128]{1,0:T(8,128)} %get-tuple-element.9.blend_ref, ...), custom_call_target="tpu_custom_call" | custom-call | tf_op jit(solution)/shard_map/pallas_call | solution.py:586
